TPU v7x, 256 devices: a whole 4x4x8 slice. The times are simulated.
256 devices in a mesh: pairs: 64 (over y, z, core), orb: 4 (over x).
Axes of the slice: x: 4, y: 4, z: 8, core: 2. Of those that a mesh axis runs over, the one named last changes fastest.
Arguments:
- amplitudes: float32 [1024, 128, 128], P(('pairs', 'orb')), may hold values from -4 to 4
- integrals: bfloat16 [1024, 128, 128], P(('pairs', 'orb')), may hold values from -6 to 6
- energies: float32 [1024, 128], P(('pairs', 'orb')), may hold values from 0.5 to 4
- intersections: bfloat16 [1024, 16, 128, 128], P(('pairs', 'orb')), may hold values from -0.5 to 0.5
- couplings: float32 [1024, 16], P(('pairs', 'orb')), may hold values from -2 to 2
- projector: float32 [1024, 128], P(('pairs', 'orb')), may hold values from -0.5 to 0.5
- pair_orbitals: int32 [1024, 2], P(('pairs', 'orb')), may hold values from 0 to 31
- coupled: int32 [1024, 16], replicated, may hold values from 0 to 1023, as said below
- pair_slot: int32 [1024], replicated, may hold values from 0 to 1023, as said below
Outputs:
- final_amplitudes: float32 [1024, 128, 128], P(('pairs', 'orb'))
- residual: float32 [1024, 128, 128], P(('pairs', 'orb'))
Inputs may be any that keep to these rules, and one draw needn't show every extreme that they name: `coupled`: each row holds 16 different pair ids, never the id of the pair held in that row's slot. The rows of one device name at most 1 different pairs held by the devices of any one pairs index, and exactly 1 held by the devices of the next pairs index. `pair_slot`: A permutation of the pair ids.
All inputs are finite; a program needn't handle non-finite values.
Results may differ from a plain program's by a relative error of at most 0.00037.
Values may be sent and summed in bfloat16 or wider, within the bound.
A program may use at most 64 MiB of HBM per device.

v0:
```python
import jax
import jax.numpy as jnp
from jax import lax
from jax.sharding import PartitionSpec as P

PAIRS_ORB = 32
ITERS = 2


def body(
    amplitudes,
    integrals,
    energies,
    intersections,
    couplings,
    projector,
    pair_orbitals,
    coupled,
    pair_slot,
):
    highest = lax.Precision.HIGHEST
    pair_count = lax.axis_size("pairs")
    orb_count = lax.axis_size("orb")
    devices = pair_count * orb_count
    per_device = amplitudes.shape[0]
    width = amplitudes.shape[1]
    total = coupled.shape[0]
    capacity = 1 + coupled.shape[1] // pair_count
    group = orb_count * per_device
    orbitals = total // PAIRS_ORB
    pair_idx = lax.axis_index("pairs")
    orb_idx = lax.axis_index("orb")
    device_id = pair_idx * orb_count + orb_idx
    targets = pair_slot[coupled]
    row_owner = jnp.broadcast_to(
        (jnp.arange(total, dtype=jnp.int32) // per_device)[:, None], targets.shape
    )
    needed = jnp.zeros((devices, total), jnp.int32).at[row_owner, targets].set(1)
    mine = lax.dynamic_slice_in_dim(needed, device_id, 1, 0)[0].reshape(pair_count, group)
    ranks = (jnp.cumsum(mine, axis=1) - 1).reshape(total)
    own_targets = lax.dynamic_slice_in_dim(targets, device_id * per_device, per_device, 0)
    slot_ids = jnp.arange(capacity, dtype=jnp.int32)
    group_cols = lax.dynamic_slice_in_dim(needed, pair_idx * group, group, 1)
    group_rank = jnp.cumsum(group_cols, axis=1) - 1
    entry_pos = own_targets // group * capacity + ranks[own_targets]
    dest_cols = group_cols.reshape(pair_count, orb_count, group)
    dest_cols = lax.dynamic_slice_in_dim(dest_cols, orb_idx, 1, 1)[:, 0]
    dest_rank = group_rank.reshape(pair_count, orb_count, group)
    dest_rank = lax.dynamic_slice_in_dim(dest_rank, orb_idx, 1, 1)[:, 0]
    select = (
        (dest_cols == 1)[:, None, :] & (dest_rank[:, None, :] == slot_ids[None, :, None])
    ).astype(jnp.bfloat16)
    orbital_ids = jnp.arange(orbitals, dtype=jnp.int32)
    first_hot = (pair_orbitals[:, 0:1] == orbital_ids[None, :]).astype(jnp.float32)
    second_hot = (pair_orbitals[:, 1:2] == orbital_ids[None, :]).astype(jnp.float32)
    denom = energies[:, :, None] + energies[:, None, :]
    state = amplitudes
    residual = amplitudes
    for step in range(ITERS):
        blocks = state.astype(jnp.bfloat16)
        group_blocks = lax.all_gather(blocks, "orb", axis=0, tiled=True)
        outgoing = jnp.einsum(
            "pcj,jxy->pcxy", select, group_blocks, preferred_element_type=jnp.float32
        )
        outgoing = outgoing.astype(jnp.bfloat16)
        arrived = lax.all_to_all(outgoing, "pairs", split_axis=0, concat_axis=0, tiled=True)
        arrived = arrived.reshape(pair_count * capacity, width, width)
        fetched = arrived[entry_pos]
        lifted = jnp.einsum(
            "pkab,pkbc->pkac", intersections, fetched, preferred_element_type=jnp.float32
        )
        scaled = (couplings[:, :, None, None] * lifted).astype(jnp.bfloat16)
        coupling = jnp.einsum(
            "pkac,pkdc->pad", scaled, intersections, preferred_element_type=jnp.float32
        )
        projected = jnp.einsum("pab,pb->pa", state, projector, precision=highest)
        partial_sum = jnp.dot(first_hot.T, projected, precision=highest) + jnp.dot(
            second_hot.T, projected, precision=highest
        )
        summed = lax.psum(partial_sum, ("pairs", "orb"))
        left = jnp.dot(first_hot, summed, precision=highest)
        right = jnp.dot(second_hot, summed, precision=highest)
        residual = (
            integrals.astype(jnp.float32)
            + energies[:, :, None] * state
            + state * energies[:, None, :]
            - coupling
            + left[:, :, None] * projector[:, None, :]
            + projector[:, :, None] * right[:, None, :]
        )
        state = state - residual / denom
    return (state, residual)


def solution(mesh):
    return jax.shard_map(
        body,
        mesh=mesh,
        in_specs=(
            P(("pairs", "orb"), None, None),
            P(("pairs", "orb"), None, None),
            P(("pairs", "orb"), None),
            P(("pairs", "orb"), None, None, None),
            P(("pairs", "orb"), None),
            P(("pairs", "orb"), None),
            P(("pairs", "orb"), None),
            P(),
            P(),
        ),
        out_specs=(P(("pairs", "orb"), None, None), P(("pairs", "orb"), None, None)),
        check_vma=False,
    )
```

profile of v0, /device:TPU:1, one launch (start us, length us, event | category | flops | bytes accessed | tf_op | source)
XLA Modules:
  0.0 392.0 jit_solution(17940552267861765877)
XLA Ops:
  0.6 0.0 copy-start
  0.7 0.6 add_select_fusion
  1.3 0.6 broadcast_compare_fusion
  1.9 0.8 compare_select_fusion.1
  2.7 0.2 copy.38
  2.9 0.2 reshape.137
  3.1 65.3 %gather_fusion = s32[16384]{0:T(1024)S(1)} fusion(s32[1024]{0:T(1024)S(1)} %copy-done.1, s32[16384]{0:T(1024)S(1)} %broadcast_clamp_fusion), kind=kCustom, calls=%fused_computation | custom fusion | bytes 196608 | tf_op jit(solution)/shard_map/gather | solution.py:34
  68.4 0.0 copy-start.3
  68.4 0.0 copy-start.4
  68.4 0.0 copy-start.9
  68.4 0.0 copy-start.8
  68.5 0.2 gather.15
  68.6 0.1 compare_select_fusion
  68.7 0.2 copy.39
  68.9 0.2 copy-done.3
  69.1 0.0 copy-done.4
  69.1 0.0 copy-done.6
  69.1 0.1 multiply_reduce_fusion
  69.2 0.1 and_reduce_fusion
  69.3 0.2 copy.40
  69.5 0.2 reshape.167
  69.7 0.0 copy-start.2
  69.8 0.6 broadcast.186
  70.4 60.8 %scatter_custom_fusion = s32[262144]{0:T(1024)S(1)} fusion(s32[16384]{0:T(1024)S(1)} %reshape.167, s32[16384]{0:T(1024)} %broadcast.186, s32[]{:T(128)} %constant.52.clone.1), kind=kCustom, calls=%fused_computation.28 | custom fusion | bytes 1049088
  131.2 1.1 reshape.134
  132.3 1.0 constant_dynamic-slice_fusion
  133.4 0.7 reduce_window_sum.22
  134.1 12.3 %all_gather.6 = bf16[16,128,128]{2,1,0:T(8,128)(2,1)S(1)} all-gather(bf16[4,128,128]{2,1,0:T(8,128)(2,1)S(1)} %convert_element_type.38), channel_id=1, replica_groups=mesh['pairs'=64,'orb'=4] {'orb'}, dimensions={0}, use_global_device_ids=true | all-gather | bytes 655360 | tf_op jit(solution)/shard_map/all_gather | solution.py:61
  146.4 0.7 convert_bitcast_fusion.1
  147.1 2.6 copy.45
  149.8 14.2 %all-to-all-start = ((bf16[64,1,128,128]{3,2,1,0:T(8,128)(2,1)}), bf16[64,1,128,128]{3,2,1,0:T(8,128)(2,1)}, u32[]{:S(2)}, u32[]{:S(2)}) async-start(bf16[64,1,128,128]{3,2,1,0:T(8,128)(2,1)} %copy.45), calls=%async_computation | async-start | bytes 4194304 | tf_op jit(solution)/shard_map/all_to_all | solution.py:66
  164.0 0.0 copy-start.7
  164.0 0.0 copy-start.5
  164.0 0.2 reshape.136
  164.2 0.8 dynamic-slice_reduce_fusion
  165.0 0.1 reshape_squeeze.3
  165.1 0.2 reduce_window_sum.23
  165.2 0.1 sub.37
  165.3 0.1 reshape.145
  165.4 0.7 gather_fusion.1
  166.2 0.1 reshape.144
  166.3 0.1 reshape.153
  166.4 0.5 fusion.65
  166.9 0.3 fusion.54
  167.2 0.3 convolution_add_fusion.1
  167.4 89.2 %psum.14 = f32[32,128]{1,0:T(8,128)S(1)} all-reduce(f32[32,128]{1,0:T(8,128)S(1)} %convolution_add_fusion.1), channel_id=1, replica_groups=mesh['pairs'=64,'orb'=4] {'pairs','orb'}, use_global_device_ids=true, to_apply=%region_3.4 | all-reduce | flops 4096 | bytes 32768 | tf_op jit(solution)/shard_map/psum | solution.py:80
  256.7 0.2 fusion.53
  256.9 0.2 fusion.50
  257.0 0.0 copy-start.11
  257.1 0.0 copy-start.12
  257.1 3.7 gather_fusion.2
  260.8 3.8 fusion.64
  264.6 11.4 %all_gather.7 = bf16[16,128,128]{2,1,0:T(8,128)(2,1)S(1)} all-gather(bf16[4,128,128]{2,1,0:T(8,128)(2,1)S(1)} %get-tuple-element.4), channel_id=1, replica_groups=mesh['pairs'=64,'orb'=4] {'orb'}, dimensions={0}, use_global_device_ids=true | all-gather | bytes 655360 | tf_op jit(solution)/shard_map/all_gather | solution.py:61
  276.1 0.7 convert_bitcast_fusion
  276.8 2.6 copy.50
  279.4 11.7 %all-to-all-start.1 = ((bf16[64,1,128,128]{3,2,1,0:T(8,128)(2,1)}), bf16[64,1,128,128]{3,2,1,0:T(8,128)(2,1)}, u32[]{:S(2)}, u32[]{:S(2)}) async-start(bf16[64,1,128,128]{3,2,1,0:T(8,128)(2,1)} %copy.50), calls=%async_computation.1 | async-start | bytes 4194304 | tf_op jit(solution)/shard_map/all_to_all | solution.py:66
  291.1 0.5 fusion.66
  291.6 0.3 fusion.52
  291.9 0.3 convolution_add_fusion
  292.2 91.1 %psum.15 = f32[32,128]{1,0:T(8,128)S(1)} all-reduce(f32[32,128]{1,0:T(8,128)S(1)} %convolution_add_fusion), channel_id=1, replica_groups=mesh['pairs'=64,'orb'=4] {'pairs','orb'}, use_global_device_ids=true, to_apply=%region_4.5 | all-reduce | flops 4096 | bytes 32768 | tf_op jit(solution)/shard_map/psum | solution.py:80
  383.3 0.2 fusion.51
  383.5 0.2 fusion.49
  383.7 3.7 gather_fusion.3
  387.4 4.6 %fusion.40 = (f32[4,128,128]{2,1,0:T(8,128)}, f32[4,128,128]{2,1,0:T(8,128)}) fusion(f32[4,128,128]{2,1,0:T(8,128)S(1)} %get-tuple-element.5, f32[4,128]{1,0:T(4,128)S(1)} %copy-done.12, f32[4,128]{1,0:T(4,128)S(1)} %fusion.49, f32[4,128]{1,0:T(4,128)S(1)} %copy-done.5, f32[4,128]{1,0:T(4,128)S(1)} %fusion.51, bf16[4,16,128,128]{3,2,1,0:T(8,128)(2,1)S(1)} %copy-done, ...), kind=kOutput, calls=%fused_computation.35 | convolution fusion | flops 539820032 | bytes 5120256 | tf_op jit(solution)/shard_map/pkac,pkdc->pad/dot_general | solution.py:73
  (27 shorter events, 0.2 us)
Async XLA Ops:
  0.6 260.2 %copy-start = (bf16[4,16,128,128]{3,2,1,0:T(8,128)(2,1)S(1)}, bf16[4,16,128,128]{3,2,1,0:T(8,128)(2,1)}, u32[]{:S(2)}) copy-start(bf16[4,16,128,128]{3,2,1,0:T(8,128)(2,1)} %param.12) | copy-start | bytes 6291460
  0.6 2.5 copy-start.1
  68.4 0.7 copy-start.3
  68.4 0.7 copy-start.4
  68.4 0.7 copy-start.6
  68.4 0.7 copy-start.9
  68.4 0.8 copy-start.8
  69.7 64.4 %copy-start.2 = (f32[4,128,128]{2,1,0:T(8,128)S(1)}, f32[4,128,128]{2,1,0:T(8,128)}, u32[]{:S(2)}) copy-start(f32[4,128,128]{2,1,0:T(8,128)} %param.9) | copy-start | bytes 786436
  149.8 107.3 %all-to-all-start = ((bf16[64,1,128,128]{3,2,1,0:T(8,128)(2,1)}), bf16[64,1,128,128]{3,2,1,0:T(8,128)(2,1)}, u32[]{:S(2)}, u32[]{:S(2)}) async-start(bf16[64,1,128,128]{3,2,1,0:T(8,128)(2,1)} %copy.45), calls=%async_computation | async-start | bytes 4194304 | tf_op jit(solution)/shard_map/all_to_all | solution.py:66
  164.0 2.4 copy-start.7
  164.0 2.4 copy-start.5
  257.0 3.8 copy-start.10
  257.0 3.8 copy-start.11
  257.1 3.8 copy-start.12
  279.4 104.3 %all-to-all-start.1 = ((bf16[64,1,128,128]{3,2,1,0:T(8,128)(2,1)}), bf16[64,1,128,128]{3,2,1,0:T(8,128)(2,1)}, u32[]{:S(2)}, u32[]{:S(2)}) async-start(bf16[64,1,128,128]{3,2,1,0:T(8,128)(2,1)} %copy.50), calls=%async_computation.1 | async-start | bytes 4194304 | tf_op jit(solution)/shard_map/all_to_all | solution.py:66
where the time goes:
time: 393 us; the launch traced here: 392 us
  blocking collectives  204 us (52%)
  local copies, waits for them, and re-layouts  145 us (37%)
  starting transfers between devices  25.9 us (7%)
  matrix products  12.6 us (3%)
    psum x2, blocking collectives, body(): summed = lax.psum(partial_sum, ('pairs', 'orb'))  180 us
    gather x3, local copies, waits for them, and re-layouts, body(): targets = pair_slot[coupled]  65.6 us
    unnamed x30, local copies, waits for them, and re-layouts  62.1 us
    all_to_all x2, starting transfers between devices, body(): lax.all_to_all(outgoing, 'pairs', split_axis=0, concat_axis=0, tiled=True)  25.9 us
    all_gather x2, blocking collectives, body(): group_blocks = lax.all_gather(blocks, 'orb', axis=0, tiled=True)  23.7 us
    dot_general x2, matrix products, body(): jnp.einsum('pkac,pkdc->pad', scaled, intersections, preferred_element_typ...  8.38 us
  transfers between devices with their start and end apart: 2, of which 0 were waited for; matrix products, arithmetic and copies ran while one was open for 1% of the time, Pallas kernels for 0%

commit v1 on v0

--- a/solution.py
+++ b/solution.py
@@ -77,7 +77,7 @@
         partial_sum = jnp.dot(first_hot.T, projected, precision=highest) + jnp.dot(
             second_hot.T, projected, precision=highest
         )
-        summed = lax.psum(partial_sum, ("pairs", "orb"))
+        summed = lax.psum(lax.psum(partial_sum, "orb"), "pairs")
         left = jnp.dot(first_hot, summed, precision=highest)
         right = jnp.dot(second_hot, summed, precision=highest)
         residual = (

time: 393 us -> 777 us (1.98)
  blocking collectives: 204 us -> 582 us
    psum x2 -> x4, blocking collectives: 180 us -> 559 us  [body(): summed = lax.psum(lax.psum(partial_sum, 'orb'), 'pairs')]
where the time goes in v1:
time: 777 us; the launch traced here: 771 us
  blocking collectives  582 us (75%)
  local copies, waits for them, and re-layouts  145 us (19%)
  starting transfers between devices  27.6 us (4%)
  matrix products  12.6 us (2%)
    psum x4, blocking collectives, body(): summed = lax.psum(lax.psum(partial_sum, 'orb'), 'pairs')  559 us
    gather x3, local copies, waits for them, and re-layouts, body(): targets = pair_slot[coupled]  65.6 us
    unnamed x30, local copies, waits for them, and re-layouts  62.1 us
    all_to_all x2, starting transfers between devices, body(): lax.all_to_all(outgoing, 'pairs', split_axis=0, concat_axis=0, tiled=True)  27.6 us
    all_gather x2, blocking collectives, body(): group_blocks = lax.all_gather(blocks, 'orb', axis=0, tiled=True)  22.4 us
  transfers between devices with their start and end apart: 2, of which 0 were waited for; matrix products, arithmetic and copies ran while one was open for 1% of the time, Pallas kernels for 0%

profile of v1, /device:TPU:1, one launch (start us, length us, event | category | flops | bytes accessed | tf_op | source)
XLA Modules:
  0.0 771.5 jit_solution(2913814473142485360)
XLA Ops:
  0.6 0.0 copy-start
  0.7 0.6 add_select_fusion
  1.3 0.6 broadcast_compare_fusion
  1.9 0.8 compare_select_fusion.1
  2.7 0.2 copy.38
  2.9 0.2 reshape.137
  3.1 65.3 %gather_fusion = s32[16384]{0:T(1024)S(1)} fusion(s32[1024]{0:T(1024)S(1)} %copy-done.1, s32[16384]{0:T(1024)S(1)} %broadcast_clamp_fusion), kind=kCustom, calls=%fused_computation | custom fusion | bytes 196608 | tf_op jit(solution)/shard_map/gather | solution.py:34
  68.4 0.0 copy-start.3
  68.4 0.0 copy-start.9
  68.4 0.0 copy-start.8
  68.5 0.2 gather.15
  68.6 0.1 compare_select_fusion
  68.7 0.2 copy.39
  68.9 0.2 copy-done.3
  69.1 0.0 copy-done.4
  69.1 0.0 copy-done.6
  69.1 0.1 multiply_reduce_fusion
  69.2 0.1 and_reduce_fusion
  69.3 0.2 copy.40
  69.5 0.2 reshape.167
  69.7 0.0 copy-start.2
  69.8 0.6 broadcast.186
  70.4 60.8 %scatter_custom_fusion = s32[262144]{0:T(1024)S(1)} fusion(s32[16384]{0:T(1024)S(1)} %reshape.167, s32[16384]{0:T(1024)} %broadcast.186, s32[]{:T(128)} %constant.52.clone.1), kind=kCustom, calls=%fused_computation.28 | custom fusion | bytes 1049088
  131.2 1.1 reshape.134
  132.3 1.0 constant_dynamic-slice_fusion
  133.4 0.7 reduce_window_sum.22
  134.1 12.3 %all_gather.6 = bf16[16,128,128]{2,1,0:T(8,128)(2,1)S(1)} all-gather(bf16[4,128,128]{2,1,0:T(8,128)(2,1)S(1)} %convert_element_type.38), channel_id=1, replica_groups=mesh['pairs'=64,'orb'=4] {'orb'}, dimensions={0}, use_global_device_ids=true | all-gather | bytes 655360 | tf_op jit(solution)/shard_map/all_gather | solution.py:61
  146.4 0.7 convert_bitcast_fusion.1
  147.1 2.6 copy.45
  149.8 14.2 %all-to-all-start = ((bf16[64,1,128,128]{3,2,1,0:T(8,128)(2,1)}), bf16[64,1,128,128]{3,2,1,0:T(8,128)(2,1)}, u32[]{:S(2)}, u32[]{:S(2)}) async-start(bf16[64,1,128,128]{3,2,1,0:T(8,128)(2,1)} %copy.45), calls=%async_computation | async-start | bytes 4194304 | tf_op jit(solution)/shard_map/all_to_all | solution.py:66
  164.0 0.0 copy-start.7
  164.0 0.0 copy-start.5
  164.0 0.2 reshape.136
  164.2 0.8 dynamic-slice_reduce_fusion
  165.0 0.1 reshape_squeeze.3
  165.1 0.2 reduce_window_sum.23
  165.2 0.1 sub.37
  165.3 0.1 reshape.145
  165.4 0.7 gather_fusion.1
  166.2 0.1 reshape.144
  166.3 0.1 reshape.153
  166.4 0.5 fusion.65
  166.9 0.3 fusion.54
  167.2 0.3 convolution_add_fusion.1
  167.4 15.0 %psum.28 = f32[32,128]{1,0:T(8,128)S(1)} all-reduce(f32[32,128]{1,0:T(8,128)S(1)} %convolution_add_fusion.1), channel_id=1, replica_groups=mesh['pairs'=64,'orb'=4] {'orb'}, use_global_device_ids=true, to_apply=%region_3.4 | all-reduce | flops 4096 | bytes 32768 | tf_op jit(solution)/shard_map/psum | solution.py:80
  182.4 263.5 %psum.29 = f32[32,128]{1,0:T(8,128)S(1)} all-reduce(f32[32,128]{1,0:T(8,128)S(1)} %psum.28), channel_id=1, replica_groups=mesh['pairs'=64,'orb'=4] {'pairs'}, use_global_device_ids=true, to_apply=%region_4.5 | all-reduce | flops 4096 | bytes 32768 | tf_op jit(solution)/shard_map/psum | solution.py:80
  445.9 0.2 fusion.53
  446.1 0.2 fusion.50
  446.3 0.0 copy-start.11
  446.3 3.7 gather_fusion.2
  450.1 3.8 fusion.64
  453.9 10.1 %all_gather.7 = bf16[16,128,128]{2,1,0:T(8,128)(2,1)S(1)} all-gather(bf16[4,128,128]{2,1,0:T(8,128)(2,1)S(1)} %get-tuple-element.4), channel_id=1, replica_groups=mesh['pairs'=64,'orb'=4] {'orb'}, dimensions={0}, use_global_device_ids=true | all-gather | bytes 655360 | tf_op jit(solution)/shard_map/all_gather | solution.py:61
  464.0 0.7 convert_bitcast_fusion
  464.7 2.6 copy.50
  467.4 13.4 %all-to-all-start.1 = ((bf16[64,1,128,128]{3,2,1,0:T(8,128)(2,1)}), bf16[64,1,128,128]{3,2,1,0:T(8,128)(2,1)}, u32[]{:S(2)}, u32[]{:S(2)}) async-start(bf16[64,1,128,128]{3,2,1,0:T(8,128)(2,1)} %copy.50), calls=%async_computation.1 | async-start | bytes 4194304 | tf_op jit(solution)/shard_map/all_to_all | solution.py:66
  480.8 0.5 fusion.66
  481.3 0.3 fusion.52
  481.6 0.3 convolution_add_fusion
  481.9 14.7 %psum.30 = f32[32,128]{1,0:T(8,128)S(1)} all-reduce(f32[32,128]{1,0:T(8,128)S(1)} %convolution_add_fusion), channel_id=1, replica_groups=mesh['pairs'=64,'orb'=4] {'orb'}, use_global_device_ids=true, to_apply=%region_5.6 | all-reduce | flops 4096 | bytes 32768 | tf_op jit(solution)/shard_map/psum | solution.py:80
  496.5 266.3 %psum.31 = f32[32,128]{1,0:T(8,128)S(1)} all-reduce(f32[32,128]{1,0:T(8,128)S(1)} %psum.30), channel_id=1, replica_groups=mesh['pairs'=64,'orb'=4] {'pairs'}, use_global_device_ids=true, to_apply=%region_6.7 | all-reduce | flops 4096 | bytes 32768 | tf_op jit(solution)/shard_map/psum | solution.py:80
  762.8 0.2 fusion.51
  763.0 0.2 fusion.49
  763.2 3.7 gather_fusion.3
  766.9 4.6 fusion.40
  (29 shorter events, 0.2 us)
Async XLA Ops:
  0.6 449.4 %copy-start = (bf16[4,16,128,128]{3,2,1,0:T(8,128)(2,1)S(1)}, bf16[4,16,128,128]{3,2,1,0:T(8,128)(2,1)}, u32[]{:S(2)}) copy-start(bf16[4,16,128,128]{3,2,1,0:T(8,128)(2,1)} %param.12) | copy-start | bytes 6291460
  0.6 2.5 copy-start.1
  68.4 0.7 copy-start.3
  68.4 0.7 copy-start.4
  68.4 0.7 copy-start.6
  68.4 0.7 copy-start.9
  68.4 0.8 copy-start.8
  69.7 64.4 %copy-start.2 = (f32[4,128,128]{2,1,0:T(8,128)S(1)}, f32[4,128,128]{2,1,0:T(8,128)}, u32[]{:S(2)}) copy-start(f32[4,128,128]{2,1,0:T(8,128)} %param.9) | copy-start | bytes 786436
  149.8 296.5 %all-to-all-start = ((bf16[64,1,128,128]{3,2,1,0:T(8,128)(2,1)}), bf16[64,1,128,128]{3,2,1,0:T(8,128)(2,1)}, u32[]{:S(2)}, u32[]{:S(2)}) async-start(bf16[64,1,128,128]{3,2,1,0:T(8,128)(2,1)} %copy.45), calls=%async_computation | async-start | bytes 4194304 | tf_op jit(solution)/shard_map/all_to_all | solution.py:66
  164.0 2.4 copy-start.7
  164.0 2.4 copy-start.5
  446.3 3.8 copy-start.10
  446.3 3.8 copy-start.11
  446.3 3.8 copy-start.12
  467.4 295.8 %all-to-all-start.1 = ((bf16[64,1,128,128]{3,2,1,0:T(8,128)(2,1)}), bf16[64,1,128,128]{3,2,1,0:T(8,128)(2,1)}, u32[]{:S(2)}, u32[]{:S(2)}) async-start(bf16[64,1,128,128]{3,2,1,0:T(8,128)(2,1)} %copy.50), calls=%async_computation.1 | async-start | bytes 4194304 | tf_op jit(solution)/shard_map/all_to_all | solution.py:66
